TPU v7x, 128 devices: a whole 4x4x4 slice. The times are simulated.
128 devices in a mesh: fsdp: 4 (over x_hi, core), ctx: 32 (over y, z, x_lo).
Axes of the slice: x: 4 (x_hi: 2, x_lo: 2; x = x_hi * 2 + x_lo), y: 4, z: 4, core: 2. Of those that a mesh axis runs over, the one named last changes fastest.
Arguments:
- query_branch: bfloat16 [4, 8192, 4096], P('fsdp', 'ctx'), may hold values from -6 to 6
- key_branch: bfloat16 [4, 8192, 4096], P('fsdp', 'ctx'), may hold values from -6 to 6
- value_branch: bfloat16 [4, 8192, 4096], P('fsdp', 'ctx'), may hold values from -6 to 6
- cotangent: bfloat16 [4, 8192, 4096], P('fsdp', 'ctx'), may hold values from -6 to 6
- quantized_weight_codes: int32 [4096, 4096], P('ctx', 'fsdp'), may hold values from 0 to 15
- scale_code_bytes: int32 [4096, 64], P('ctx', 'fsdp'), may hold values from 0 to 255
- row_scale_second: float32 [4096], P('ctx'), may hold values from 0.01 to 0.1
- filters: bfloat16 [256, 128], replicated, may hold values from -0.5 to 0.5
- channel_skip_weight: float32 [4096], replicated, may hold values from -6 to 6
- adapter_down_weight: bfloat16 [4096, 64], P('ctx'), may hold values from -0.09375 to 0.09375
- adapter_up_weight: bfloat16 [64, 4096], P(None, 'fsdp'), may hold values from -0.75 to 0.75
Outputs:
- output: bfloat16 [4, 8192, 4096], P('fsdp', 'ctx')
- grad_query: bfloat16 [4, 8192, 4096], P('fsdp', 'ctx')
- grad_key: bfloat16 [4, 8192, 4096], P('fsdp', 'ctx')
- grad_value: bfloat16 [4, 8192, 4096], P('fsdp', 'ctx')
- grad_down: bfloat16 [4096, 64], P('ctx')
- grad_up: bfloat16 [64, 4096], P(None, 'fsdp')
All inputs are finite; a program needn't handle non-finite values.
Results may differ from a plain program's by a relative error of at most 0.0067.
Values may be sent and summed in bfloat16 or wider, within the bound.
No kernel may reach another device: no remote copies, remote signals or barrier semaphores. Data moves between devices by JAX's collectives and lax.ppermute only.
A program may use at most 256 MiB of HBM per device.

v0:
```python
import math
import jax
import jax.numpy as jnp
from jax import lax
from jax.sharding import PartitionSpec as P

QBLOCK = 64
normal_levels = (
    -1.0,
    -0.6961928009986877,
    -0.5250730514526367,
    -0.39491748809814453,
    -0.28444138169288635,
    -0.18477343022823334,
    -0.09105003625154495,
    0.0,
    0.07958029955625534,
    0.16093020141124725,
    0.24611230194568634,
    0.33791524171829224,
    0.44070982933044434,
    0.5626170039176941,
    0.7229568362236023,
    1.0,
)
adapter_scale = 0.25


def from_behind(shard, axis, by):
    count = lax.axis_size(axis)
    pairs = [(i, i + by) for i in range(count) if 0 <= i + by < count]
    return lax.ppermute(shard, axis, pairs)


def dequantize(quantized_weight_codes, scale_code_bytes, row_scale_second):
    levels = jnp.zeros(quantized_weight_codes.shape, jnp.float32)
    for number in range(16):
        levels = jnp.where(quantized_weight_codes == number, normal_levels[number], levels)
    absmax = row_scale_second[:, None] * (scale_code_bytes.astype(jnp.float32) + 1.0) / 256.0
    absmax = jnp.repeat(absmax, QBLOCK, axis=1)
    return (levels * absmax).astype(jnp.bfloat16)


def toeplitz(filter_taps, filter_len):
    groups = filter_taps.shape[0]
    padded = jnp.concatenate([filter_taps, jnp.zeros((groups, filter_len), filter_taps.dtype)], 1)
    repeated = jnp.tile(padded, (1, filter_len))[:, : filter_len * (2 * filter_len - 1)]
    return repeated.reshape(groups, filter_len, 2 * filter_len - 1)


def block_conv(extended, toep, filter_len):
    row_count = extended.shape[0] - (filter_len - 1)
    blocks = row_count // filter_len
    current = extended[:row_count].reshape(blocks, filter_len, -1)
    following = jnp.concatenate(
        [extended[filter_len:], jnp.zeros((1, extended.shape[1]), extended.dtype)], 0
    )
    following = following.reshape(blocks, filter_len, -1)[:, : filter_len - 1]
    windows = jnp.concatenate([current, following], 1)
    windows = windows.reshape(blocks, 2 * filter_len - 1, toep.shape[0], -1)
    result = jnp.einsum("gts,bsgk->btgk", toep, windows, preferred_element_type=jnp.float32)
    return result.reshape(row_count, -1)


def local(
    query_branch,
    key_branch,
    value_branch,
    cotangent,
    quantized_weight_codes,
    scale_code_bytes,
    row_scale_second,
    filters,
    channel_skip_weight,
    adapter_down_weight,
    adapter_up_weight,
):
    filter_len = filters.shape[1]
    queries = query_branch[0]
    output_gradient = cotangent[0]
    row_count, channels = queries.shape
    token_count = query_branch.shape[0] * row_count * lax.axis_size("ctx") * lax.axis_size("fsdp")
    multiplier = adapter_scale / math.sqrt(token_count)
    query_float = queries.astype(jnp.float32)
    key_float = key_branch[0].astype(jnp.float32)
    value_float = value_branch[0].astype(jnp.float32)
    mixed = (key_float * value_float).astype(jnp.bfloat16)
    before = from_behind(mixed[row_count - (filter_len - 1) :], "ctx", 1)
    ahead_toep = toeplitz(jnp.flip(filters, 1), filter_len)
    back_toep = toeplitz(filters, filter_len)
    gated = block_conv(
        jnp.concatenate([before, mixed], 0), ahead_toep, filter_len
    ) + channel_skip_weight * mixed.astype(jnp.float32)
    gated_signal = (query_float * gated).astype(jnp.bfloat16)
    local_piece = dequantize(quantized_weight_codes, scale_code_bytes, row_scale_second)
    local_rows, up_complete = (
        lax.all_gather(local_piece, "fsdp", axis=1, tiled=True),
        lax.all_gather(adapter_up_weight, "fsdp", axis=1, tiled=True),
    )
    backward_up_term = jnp.einsum(
        "td,rd->tr", output_gradient, up_complete, preferred_element_type=jnp.float32
    ).astype(jnp.bfloat16)
    weight_rows = lax.all_gather(local_rows, "ctx", axis=0, tiled=True)
    rank_rows = lax.all_gather(adapter_down_weight, "ctx", axis=0, tiled=True)
    output_total = jnp.dot(gated_signal, weight_rows, preferred_element_type=jnp.float32)
    down_sum = jnp.dot(gated_signal, rank_rows, preferred_element_type=jnp.float32)
    elementwise_product = jnp.einsum(
        "td,cd->tc", output_gradient, weight_rows, preferred_element_type=jnp.float32
    )
    elementwise_product = elementwise_product + adapter_scale * jnp.einsum(
        "tr,cr->tc", backward_up_term, rank_rows, preferred_element_type=jnp.float32
    )
    down_projection = down_sum.astype(jnp.bfloat16)
    output = (
        output_total
        + adapter_scale * jnp.dot(down_projection, up_complete, preferred_element_type=jnp.float32)
    ).astype(jnp.bfloat16)
    grad_query = (elementwise_product * gated).astype(jnp.bfloat16)
    grad_gated = (elementwise_product * query_float).astype(jnp.bfloat16)
    leading = jnp.concatenate(
        [jnp.zeros((filter_len, channels), jnp.bfloat16), grad_gated[: filter_len - 1]], 0
    )
    spill = block_conv(leading, back_toep, filter_len)
    arrived = from_behind(spill[1:], "ctx", -1)
    tail_rows = jnp.concatenate(
        [grad_gated, jnp.zeros((filter_len - 1, channels), jnp.bfloat16)], 0
    )
    local_grad = block_conv(tail_rows, back_toep, filter_len)
    local_grad = local_grad + jnp.concatenate(
        [jnp.zeros((row_count - filter_len + 1, channels), jnp.float32), arrived], 0
    )
    grad_mixed = local_grad + channel_skip_weight * grad_gated.astype(jnp.float32)
    grad_key = (grad_mixed * value_float).astype(jnp.bfloat16)
    grad_value = (grad_mixed * key_float).astype(jnp.bfloat16)
    term_down = multiplier * jnp.einsum(
        "tc,tr->cr", gated_signal, backward_up_term, preferred_element_type=jnp.float32
    )
    term_up = multiplier * jnp.einsum(
        "tr,td->rd", down_projection, output_gradient, preferred_element_type=jnp.float32
    )
    total_down = lax.psum(term_down, "fsdp")
    grad_down = lax.psum_scatter(total_down, "ctx", scatter_dimension=0, tiled=True)
    total_up = lax.psum(term_up, "ctx")
    grad_up = lax.psum_scatter(total_up, "fsdp", scatter_dimension=1, tiled=True)
    return (
        output[None],
        grad_query[None],
        grad_key[None],
        grad_value[None],
        grad_down.astype(jnp.bfloat16),
        grad_up.astype(jnp.bfloat16),
    )


def solution(mesh):
    return jax.shard_map(
        local,
        mesh=mesh,
        in_specs=(
            P("fsdp", "ctx", None),
            P("fsdp", "ctx", None),
            P("fsdp", "ctx", None),
            P("fsdp", "ctx", None),
            P("ctx", "fsdp"),
            P("ctx", "fsdp"),
            P("ctx"),
            P(),
            P(),
            P("ctx", None),
            P(None, "fsdp"),
        ),
        out_specs=(
            P("fsdp", "ctx", None),
            P("fsdp", "ctx", None),
            P("fsdp", "ctx", None),
            P("fsdp", "ctx", None),
            P("ctx", None),
            P(None, "fsdp"),
        ),
        check_vma=False,
    )
```

profile of v0, /device:TPU:1, one launch (start us, length us, event | category | flops | bytes accessed | tf_op | source)
XLA Modules:
  0.0 1086.2 jit_solution(9586040226539737358)
XLA Ops:
  10.7 24.5 %all-gather.3.cloned.1.call-done = bf16[128,4096]{0,1:T(8,128)(2,1)} async-done(((bf16[128,1024]{0,1:T(8,128)(2,1)}), bf16[128,4096]{0,1:T(8,128)(2,1)}) %all-gather.3.cloned.1.call-update) | async-done | bytes 1048592 | tf_op jit(solution)/shard_map/all_gather | solution.py:97
  46.3 41.7 %copy.62 = bf16[32,8,128,256]{3,1,2,0:T(8,128)(2,1)S(1)} copy(bf16[32,8,128,256]{3,2,1,0:T(8,128)(2,1)S(1)} %bitcast.101) | data formatting | bytes 33554432
  88.0 6.6 slice.54
  94.6 56.8 %reshape.84 = bf16[256,128,255,1]{2,1,0,3:T(8,128)(2,1)} reshape(bf16[256,32640]{1,0:T(8,128)(2,1)} %slice.54) | data formatting | bytes 33423360 | tf_op jit(solution)/shard_map/reshape | solution.py:48
  151.3 56.7 %reshape.76 = bf16[256,128,255]{2,1,0:T(8,128)(2,1)} reshape(bf16[256,32640]{1,0:T(8,128)(2,1)} %slice.54) | data formatting | bytes 33423360 | tf_op jit(solution)/shard_map/reshape | solution.py:48
  209.3 41.7 %copy.60 = bf16[32,8,128,256]{3,1,2,0:T(8,128)(2,1)S(1)} copy(bf16[32,8,128,256]{3,2,1,0:T(8,128)(2,1)S(1)} %bitcast.102) | data formatting | bytes 33554432
  251.0 6.6 slice.52
  257.6 56.8 %reshape.83 = bf16[256,128,255,1]{2,1,0,3:T(8,128)(2,1)} reshape(bf16[256,32640]{1,0:T(8,128)(2,1)} %slice.52) | data formatting | bytes 33423360 | tf_op jit(solution)/shard_map/reshape | solution.py:48
  317.6 4.2 copy.57
  321.8 12.4 %all_gather.15 = bf16[64,4096]{1,0:T(8,128)(2,1)S(1)} all-gather(bf16[64,1024]{1,0:T(8,128)(2,1)S(1)} %copy-done.11), channel_id=1, replica_groups=mesh['fsdp'=4,'ctx'=32] {'fsdp'}, dimensions={1}, use_global_device_ids=true | all-gather | bytes 655360 | tf_op jit(solution)/shard_map/all_gather | solution.py:98
  334.1 80.4 %all_gather.14 = bf16[4096,64]{0,1:T(8,128)(2,1)S(1)} all-gather(bf16[128,64]{0,1:T(8,128)(2,1)S(1)} %copy-done.13), channel_id=1, replica_groups=mesh['fsdp'=4,'ctx'=32] {'ctx'}, dimensions={0}, use_global_device_ids=true | all-gather | bytes 540672 | tf_op jit(solution)/shard_map/all_gather | solution.py:104
  429.7 9.5 fusion.19
  443.6 5.7 copy.28
  449.2 329.5 %all-gather.5.cloned.1.call-done = bf16[4096,4096]{0,1:T(8,128)(2,1)} async-done(((bf16[128,4096]{0,1:T(8,128)(2,1)}), bf16[4096,4096]{0,1:T(8,128)(2,1)}) %all-gather.5.cloned.1.call-update) | async-done | bytes 33554448 | tf_op jit(solution)/shard_map/all_gather | solution.py:103
  778.8 17.2 %convolution_bitcast_fusion = f32[256,4096]{1,0:T(8,128)} fusion(bf16[4096,4096]{0,1:T(8,128)(2,1)} %all-gather.5.cloned.1.call-done, bf16[1,256,4096]{2,1,0:T(8,128)(2,1)S(1)} %copy-done), kind=kOutput, calls=%fused_computation.4 | convolution fusion | flops 8589934592 | bytes 39845888 | tf_op jit(solution)/shard_map/td,cd->tc/dot_general | solution.py:107
  796.0 6.7 fusion.29
  814.0 12.6 %convolution_bitcast_fusion.1 = f32[1,128,256,16]{1,3,2,0:T(8,128)} fusion(bf16[255,256,16]{0,2,1:T(8,128)(2,1)} %bitcast.111, bf16[256,128,255]{2,1,0:T(8,128)(2,1)} %reshape.76), kind=kOutput, calls=%fused_computation.45 | convolution fusion | flops 267386880 | bytes 20897792 | tf_op jit(solution)/shard_map/gts,bsgk->btgk/dot_general | solution.py:61
  837.6 17.7 %fusion.43 = f32[256,4096]{1,0:T(8,128)} fusion(bf16[256,4096]{1,0:T(8,128)(2,1)} %copy-done.6, bf16[4096,4096]{0,1:T(8,128)(2,1)} %all-gather.5.cloned.1.call-done), kind=kOutput, calls=%fused_computation.55 | convolution fusion | flops 8589934592 | bytes 39845888 | tf_op jit(solution)/shard_map/dot_general | solution.py:105
  872.5 9.9 fusion.24
  886.9 5.7 copy.53
  892.5 4.4 fusion.7
  896.9 6.5 fusion.30
  903.4 135.5 %all-reduce.8 = bf16[64,1024]{1,0:T(8,128)(2,1)} all-reduce(f32[64,1024]{1,0:T(8,128)} %reduce-scatter.5.cloned.1.call-done), channel_id=1, replica_groups=mesh['fsdp'=4,'ctx'=32] {'ctx'}, use_global_device_ids=true, to_apply=%region_2.3 | all-reduce | flops 65536 | bytes 393216 | tf_op jit(solution)/shard_map/psum | solution.py:143
  1038.9 40.4 %psum.16 = bf16[128,64]{0,1:T(8,128)(2,1)} all-reduce(f32[128,64]{0,1:T(8,128)} %reduce-scatter.3.cloned.1.call-done), channel_id=1, replica_groups=mesh['fsdp'=4,'ctx'=32] {'fsdp'}, use_global_device_ids=true, to_apply=%region_0.1 | all-reduce | flops 8192 | bytes 49152 | tf_op jit(solution)/shard_map/psum | solution.py:141
  (79 shorter events, 82.4 us)
Async XLA Ops:
  7.2 407.4 %copy-start = (bf16[1,256,4096]{2,1,0:T(8,128)(2,1)S(1)}, bf16[1,256,4096]{2,1,0:T(8,128)(2,1)}, u32[]{:S(2)}) copy-start(bf16[1,256,4096]{2,1,0:T(8,128)(2,1)} %param.14) | copy-start | bytes 6291460
  7.2 28.0 %all-gather.3.cloned.1.call-start = ((), (), s32[]{:S(2)}) async-start(), calls=%async_computation.2 | async-start | bytes 1310720 | tf_op jit(solution)/shard_map/all_gather | solution.py:97
  10.6 768.1 %all-gather.5.cloned.1.call-start = ((), (), s32[]{:S(2)}) async-start(), calls=%async_computation.3 | async-start | bytes 34603008 | tf_op jit(solution)/shard_map/all_gather | solution.py:103
  35.2 868.2 %reduce-scatter.5.cloned.1.call-start = ((), (), s32[]{:S(2)}) async-start(), calls=%async_computation.5 | async-start | bytes 1310720 | tf_op jit(solution)/shard_map/reduce_scatter | solution.py:144
  38.2 4.7 copy-start.3
  38.2 6.5 copy-start.10
  39.8 375.6 %collective-permute-start = (bf16[127,4096]{1,0:T(8,128)(2,1)}, bf16[127,4096]{1,0:T(8,128)(2,1)}, u32[]{:S(2)}, u32[]{:S(2)}) collective-permute-start(bf16[127,4096]{1,0:T(8,128)(2,1)} %slice.49), channel_id=1, source_target_pairs={{0,1},{1,2},{2,3},{3,4},{4,5},{5,6},{6,7},{7,8},{8,9},{9,10},{10,1... | collective-permute-start | bytes 3121160 | tf_op jit(solution)/shard_map/ppermute | solution.py:32
  314.4 7.4 copy-start.11
  314.4 19.7 %copy-start.13 = (bf16[128,64]{0,1:T(8,128)(2,1)S(1)}, bf16[128,64]{0,1:T(8,128)(2,1)}, u32[]{:S(2)}) copy-start(bf16[128,64]{0,1:T(8,128)(2,1)} %param.20) | copy-start | bytes 49156
  321.8 93.6 %copy-start.4 = (bf16[256,4096]{1,0:T(8,128)(2,1)S(1)}, bf16[256,4096]{1,0:T(8,128)(2,1)}, u32[]{:S(2)}) copy-start(bf16[256,4096]{1,0:T(8,128)(2,1)} %copy-done.3) | copy-start | bytes 6291460
  426.3 3.4 copy-start.7
  449.2 346.7 %copy-start.12 = (f32[4096]{0:T(1024)S(1)}, f32[4096]{0:T(1024)}, u32[]{:S(2)}) copy-start(f32[4096]{0:T(1024)} %param.19) | copy-start | bytes 49156
  778.8 17.2 %copy-start.5 = (bf16[256,4096]{1,0:T(8,128)(2,1)S(1)}, bf16[256,4096]{1,0:T(8,128)(2,1)}, u32[]{:S(2)}) copy-start(bf16[256,4096]{1,0:T(8,128)(2,1)} %copy-done.3) | copy-start | bytes 6291460
  778.8 17.2 %copy-start.9 = (f32[256,4096]{1,0:T(8,128)S(1)}, f32[256,4096]{1,0:T(8,128)}, u32[]{:S(2)}) copy-start(f32[256,4096]{1,0:T(8,128)} %copy.28) | copy-start | bytes 12582916
  802.7 1.3 copy-start.6
  802.7 3.8 copy-start.14
  806.2 232.7 %reduce-scatter.3.cloned.1.call-start = ((), (), s32[]{:S(2)}) async-start(), calls=%async_computation.4 | async-start | bytes 1081344 | tf_op jit(solution)/shard_map/reduce_scatter | solution.py:142
  833.2 63.7 %collective-permute-start.1 = (f32[127,4096]{1,0:T(8,128)}, f32[127,4096]{1,0:T(8,128)}, u32[]{:S(2)}, u32[]{:S(2)}) collective-permute-start(f32[127,4096]{1,0:T(8,128)} %copy.52), channel_id=1, source_target_pairs={{1,0},{2,1},{3,2},{4,3},{5,4},{6,5},{7,6},{8,7},{9,8},{10,9},{11,1... | collective-permute-start | bytes 6242312 | tf_op jit(solution)/shard_map/ppermute | solution.py:32
  863.3 3.3 copy-start.1
  892.5 4.4 copy-start.2
  892.5 4.4 copy-start.8
Sparse Core Ops, SparseCore 0:
  10.8 24.3 all-gather.2
  36.7 742.0 all-gather.4
  806.4 30.7 reduce-scatter.4
  839.4 139.4 reduce-scatter.2
where the time goes:
time: 1100 us; the launch traced here: 1090 us
  waiting for transfers between devices  354 us (32%)
  local copies, waits for them, and re-layouts  344 us (31%)
  blocking collectives  269 us (24%)
  matrix products  84 us (8%)
  other arithmetic  16.8 us (2%)
  between operations  14.3 us (1%)
    all_gather x1, waiting for transfers between devices, local(): weight_rows = lax.all_gather(local_rows, 'ctx', axis=0, tiled=True)  330 us
    reshape x3, local copies, waits for them, and re-layouts, toeplitz(): return repeated.reshape(groups, filter_len, 2 * filter_len - 1)  170 us
    psum x1, blocking collectives, local(): total_up = lax.psum(term_up, 'ctx')  135 us
    unnamed x38, local copies, waits for them, and re-layouts  101 us
    all_gather x1, blocking collectives, local(): rank_rows = lax.all_gather(adapter_down_weight, 'ctx', axis=0, tiled=True)  80.4 us
    psum x1, blocking collectives, local(): total_down = lax.psum(term_down, 'fsdp')  40.4 us
    dot_general x3, matrix products, block_conv(): jnp.einsum('gts,bsgk->btgk', toep, windows, preferred_element_type=jnp.fl...  32 us
    all_gather x1, waiting for transfers between devices, local(): lax.all_gather(local_piece, 'fsdp', axis=1, tiled=True)  24.5 us
  transfers between devices with their start and end apart: 6, of which 2 were waited for; matrix products, arithmetic and copies ran while one was open for 38% of the time, Pallas kernels for 0%

commit v1 on v0

--- a/solution.py
+++ b/solution.py
@@ -101,7 +101,9 @@
         "td,rd->tr", output_gradient, up_complete, preferred_element_type=jnp.float32
     ).astype(jnp.bfloat16)
     weight_rows = lax.all_gather(local_rows, "ctx", axis=0, tiled=True)
-    rank_rows = lax.all_gather(adapter_down_weight, "ctx", axis=0, tiled=True)
+    rank_rows = jnp.concatenate(
+        lax.all_to_all(jnp.stack([adapter_down_weight] * lax.axis_size("ctx")), "ctx", 0, 0), axis=0
+    )
     output_total = jnp.dot(gated_signal, weight_rows, preferred_element_type=jnp.float32)
     down_sum = jnp.dot(gated_signal, rank_rows, preferred_element_type=jnp.float32)
     elementwise_product = jnp.einsum(

time: 1100 us -> 1190 us (1.082); the launches traced: 1090 us -> 1190 us
  waiting for transfers between devices: 354 us -> 500 us
  blocking collectives: 269 us -> 199 us
  local copies, waits for them, and re-layouts: 344 us -> 358 us
    all_gather x1, waiting for transfers between devices: 330 us -> 420 us  [local(): weight_rows = lax.all_gather(local_rows, 'ctx', axis=0, tiled=True)]
    all_gather x1 -> x0, blocking collectives: 80.4 us -> none  [local(): rank_rows = lax.all_gather(adapter_down_weight, 'ctx', axis=0, tiled=True)]
    reduce_scatter x1, waiting for transfers between devices: 0.01 us -> 79.7 us  [local(): lax.psum_scatter(total_down, 'ctx', scatter_dimension=0, tiled=True)]
    all_gather x1, waiting for transfers between devices: 24.5 us -> 0.02 us  [local(): lax.all_gather(local_piece, 'fsdp', axis=1, tiled=True)]
    psum x1, blocking collectives: 135 us -> 148 us  [local(): total_up = lax.psum(term_up, 'ctx')]
    reshape x2 -> x4, local copies, waits for them, and re-layouts: 11.3 us -> 23.5 us  [block_conv(): return result.reshape(row_count, -1)]
    unnamed x38 -> x48, local copies, waits for them, and re-layouts: 101 us -> 101 us
  transfers between devices with their start and end apart: 6 -> 7, of which waited for: 2 -> 2; matrix products, arithmetic and copies ran while one was open for 38% -> 34% of each run, Pallas kernels for 0% -> 0%
where the time goes in v1:
time: 1190 us
  waiting for transfers between devices  500 us (42%)
  local copies, waits for them, and re-layouts  358 us (30%)
  blocking collectives  199 us (17%)
  matrix products  87.3 us (7%)
  starting transfers between devices  15.5 us (1%)
  other arithmetic  15.4 us (1%)
  between operations  14.3 us (1%)
    all_gather x1, waiting for transfers between devices, local(): weight_rows = lax.all_gather(local_rows, 'ctx', axis=0, tiled=True)  420 us
    reshape x3, local copies, waits for them, and re-layouts, toeplitz(): return repeated.reshape(groups, filter_len, 2 * filter_len - 1)  170 us
    psum x1, blocking collectives, local(): total_up = lax.psum(term_up, 'ctx')  148 us
    unnamed x48, local copies, waits for them, and re-layouts  101 us
    reduce_scatter x1, waiting for transfers between devices, local(): lax.psum_scatter(total_down, 'ctx', scatter_dimension=0, tiled=True)  79.7 us
    psum x1, blocking collectives, local(): total_down = lax.psum(term_down, 'fsdp')  38.1 us
    dot_general x3, matrix products, block_conv(): jnp.einsum('gts,bsgk->btgk', toep, windows, preferred_element_type=jnp.fl...  31.2 us
  transfers between devices with their start and end apart: 7, of which 2 were waited for; matrix products, arithmetic and copies ran while one was open for 34% of the time, Pallas kernels for 0%

profile of v1, /device:TPU:1, one launch (start us, length us, event | category | flops | bytes accessed | tf_op | source)
XLA Modules:
  0.0 1190.1 jit_solution(15048625238681174294)
XLA Ops:
  20.6 8.0 all-to-all-start
  33.8 41.7 %copy.132 = bf16[32,8,128,256]{3,1,2,0:T(8,128)(2,1)S(1)} copy(bf16[32,8,128,256]{3,2,1,0:T(8,128)(2,1)S(1)} %bitcast.141) | data formatting | bytes 33554432
  75.5 6.5 slice.52
  82.1 56.7 %reshape.99 = bf16[256,128,255,1]{2,1,0,3:T(8,128)(2,1)} reshape(bf16[256,32640]{1,0:T(8,128)(2,1)} %slice.52) | data formatting | bytes 33423360 | tf_op jit(solution)/shard_map/reshape | solution.py:48
  160.6 9.5 fusion.26
  174.3 6.5 reshape.89
  180.8 5.6 copy.114
  196.0 41.7 %copy.134 = bf16[32,8,128,256]{3,1,2,0:T(8,128)(2,1)S(1)} copy(bf16[32,8,128,256]{3,2,1,0:T(8,128)(2,1)S(1)} %bitcast.142) | data formatting | bytes 33554432
  237.7 6.6 slice.54
  244.3 56.7 %reshape.100 = bf16[256,128,255,1]{2,1,0,3:T(8,128)(2,1)} reshape(bf16[256,32640]{1,0:T(8,128)(2,1)} %slice.54) | data formatting | bytes 33423360 | tf_op jit(solution)/shard_map/reshape | solution.py:48
  301.1 56.8 %reshape.92 = bf16[256,128,255]{2,1,0:T(8,128)(2,1)} reshape(bf16[256,32640]{1,0:T(8,128)(2,1)} %slice.54) | data formatting | bytes 33423360 | tf_op jit(solution)/shard_map/reshape | solution.py:48
  357.8 13.1 %all_gather.11 = bf16[64,4096]{1,0:T(8,128)(2,1)S(1)} all-gather(bf16[64,1024]{1,0:T(8,128)(2,1)S(1)} %copy-done.15), channel_id=1, replica_groups=mesh['fsdp'=4,'ctx'=32] {'fsdp'}, dimensions={1}, use_global_device_ids=true | all-gather | bytes 655360 | tf_op jit(solution)/shard_map/all_gather | solution.py:98
  376.1 5.7 copy.96
  381.9 148.0 %all-reduce.8 = bf16[64,1024]{1,0:T(8,128)(2,1)} all-reduce(f32[64,1024]{1,0:T(8,128)} %reduce-scatter.5.cloned.1.call-done), channel_id=1, replica_groups=mesh['fsdp'=4,'ctx'=32] {'ctx'}, use_global_device_ids=true, to_apply=%region_2.3 | all-reduce | flops 65536 | bytes 393216 | tf_op jit(solution)/shard_map/psum | solution.py:145
  529.8 419.9 %all-gather.5.cloned.1.call-done = bf16[4096,4096]{0,1:T(8,128)(2,1)} async-done(((bf16[128,4096]{0,1:T(8,128)(2,1)}), bf16[4096,4096]{0,1:T(8,128)(2,1)}) %all-gather.5.cloned.1.call-update) | async-done | bytes 33554448 | tf_op jit(solution)/shard_map/all_gather | solution.py:103
  949.8 17.2 %convolution_bitcast_fusion = f32[256,4096]{1,0:T(8,128)} fusion(bf16[4096,4096]{0,1:T(8,128)(2,1)} %all-gather.5.cloned.1.call-done, bf16[1,256,4096]{2,1,0:T(8,128)(2,1)S(1)} %copy-done), kind=kOutput, calls=%fused_computation.4 | convolution fusion | flops 8589934592 | bytes 39845888 | tf_op jit(solution)/shard_map/td,cd->tc/dot_general | solution.py:109
  967.0 6.2 fusion.36
  979.5 12.2 %convolution_bitcast_fusion.1 = f32[1,128,256,16]{1,3,2,0:T(8,128)} fusion(bf16[255,256,16]{0,2,1:T(8,128)(2,1)} %bitcast.151, bf16[256,128,255]{2,1,0:T(8,128)(2,1)} %reshape.92), kind=kOutput, calls=%fused_computation.54 | convolution fusion | flops 267386880 | bytes 20897792 | tf_op jit(solution)/shard_map/gts,bsgk->btgk/dot_general | solution.py:61
  1002.8 17.6 %fusion.62 = f32[256,4096]{1,0:T(8,128)} fusion(bf16[256,4096]{1,0:T(8,128)(2,1)} %get-tuple-element.9, bf16[4096,4096]{0,1:T(8,128)(2,1)} %all-gather.5.cloned.1.call-done), kind=kOutput, calls=%fused_computation.68 | convolution fusion | flops 8589934592 | bytes 39845888 | tf_op jit(solution)/shard_map/dot_general | solution.py:107
  1034.9 9.5 fusion.31
  1048.9 5.6 copy.124
  1059.0 6.6 fusion.38
  1065.5 79.7 %reduce-scatter.3.cloned.1.call-done = f32[128,64]{0,1:T(8,128)} async-done(((f32[4096,64]{0,1:T(8,128)}), f32[128,64]{0,1:T(8,128)}) %reduce-scatter.3.cloned.1.call-update) | async-done | bytes 32784 | tf_op jit(solution)/shard_map/reduce_scatter | solution.py:144
  1145.2 38.1 %psum.16 = bf16[128,64]{0,1:T(8,128)(2,1)} all-reduce(f32[128,64]{0,1:T(8,128)} %reduce-scatter.3.cloned.1.call-done), channel_id=1, replica_groups=mesh['fsdp'=4,'ctx'=32] {'fsdp'}, use_global_device_ids=true, to_apply=%region_0.1 | all-reduce | flops 8192 | bytes 49152 | tf_op jit(solution)/shard_map/psum | solution.py:143
  (93 shorter events, 100.0 us)
Async XLA Ops:
  7.2 184.7 %copy-start = (bf16[1,256,4096]{2,1,0:T(8,128)(2,1)S(1)}, bf16[1,256,4096]{2,1,0:T(8,128)(2,1)}, u32[]{:S(2)}) copy-start(bf16[1,256,4096]{2,1,0:T(8,128)(2,1)} %param.14) | copy-start | bytes 6291460
  7.2 10.9 copy-start.12
  7.2 11.1 copy-start.17
  7.2 11.1 copy-start.19
  7.2 12.4 %copy-start.16 = (bf16[128,64]{0,1:T(8,128)(2,1)S(1)}, bf16[128,64]{0,1:T(8,128)(2,1)}, u32[]{:S(2)}) copy-start(bf16[128,64]{0,1:T(8,128)(2,1)} %param.20) | copy-start | bytes 49156
  7.2 186.2 %all-gather.3.cloned.1.call-start = ((), (), s32[]{:S(2)}) async-start(), calls=%async_computation.3 | async-start | bytes 1310720 | tf_op jit(solution)/shard_map/all_gather | solution.py:97
  13.0 19.3 %copy-start.13 = (bf16[256,128]{1,0:T(8,128)(2,1)S(1)}, bf16[256,128]{1,0:T(8,128)(2,1)}, u32[]{:S(2)}) copy-start(bf16[256,128]{1,0:T(8,128)(2,1)} %param.18) | copy-start | bytes 196612
  13.0 133.0 %collective-permute-start = (bf16[127,4096]{1,0:T(8,128)(2,1)}, bf16[127,4096]{1,0:T(8,128)(2,1)}, u32[]{:S(2)}, u32[]{:S(2)}) collective-permute-start(bf16[127,4096]{1,0:T(8,128)(2,1)} %slice.49), channel_id=1, source_target_pairs={{0,1},{1,2},{2,3},{3,4},{4,5},{5,6},{6,7},{7,8},{8,9},{9,10},{10,1... | collective-permute-start | bytes 3121160 | tf_op jit(solution)/shard_map/ppermute | solution.py:32
  20.6 165.9 %all-to-all-start = ((bf16[32,128,64]{1,2,0:T(8,128)(2,1)}), bf16[32,128,64]{1,2,0:T(8,128)(2,1)S(1)}, u32[]{:S(2)}, u32[]{:S(2)}) async-start(bf16[32,128,64]{1,2,0:T(8,128)(2,1)} %stack.2), calls=%async_computation | async-start | bytes 1048576 | tf_op jit(solution)/shard_map/all_to_all | solution.py:105
  28.5 353.3 %reduce-scatter.5.cloned.1.call-start = ((), (), s32[]{:S(2)}) async-start(), calls=%async_computation.6 | async-start | bytes 1310720 | tf_op jit(solution)/shard_map/reduce_scatter | solution.py:146
  180.8 5.6 copy-start.14
  186.4 5.5 copy-start.11
  193.4 756.4 %all-gather.5.cloned.1.call-start = ((), (), s32[]{:S(2)}) async-start(), calls=%async_computation.4 | async-start | bytes 34603008 | tf_op jit(solution)/shard_map/all_gather | solution.py:103
  194.1 951.1 %reduce-scatter.3.cloned.1.call-start = ((), (), s32[]{:S(2)}) async-start(), calls=%async_computation.5 | async-start | bytes 1081344 | tf_op jit(solution)/shard_map/reduce_scatter | solution.py:144
  301.1 56.8 %copy-start.15 = (bf16[64,1024]{1,0:T(8,128)(2,1)S(1)}, bf16[64,1024]{1,0:T(8,128)(2,1)}, u32[]{:S(2)}) copy-start(bf16[64,1024]{1,0:T(8,128)(2,1)} %param.21) | copy-start | bytes 393220
  949.8 17.2 %copy-start.3 = (bf16[256,4096]{1,0:T(8,128)(2,1)S(1)}, bf16[256,4096]{1,0:T(8,128)(2,1)}, u32[]{:S(2)}) copy-start(bf16[256,4096]{1,0:T(8,128)(2,1)} %copy-done.2) | copy-start | bytes 6291460
  949.8 17.2 %copy-start.9 = (f32[256,4096]{1,0:T(8,128)S(1)}, f32[256,4096]{1,0:T(8,128)}, u32[]{:S(2)}) copy-start(f32[256,4096]{1,0:T(8,128)} %copy.96) | copy-start | bytes 12582916
  949.8 17.2 %copy-start.10 = (bf16[1,256,4096]{2,1,0:T(8,128)(2,1)S(1)}, bf16[1,256,4096]{2,1,0:T(8,128)(2,1)}, u32[]{:S(2)}) copy-start(bf16[1,256,4096]{2,1,0:T(8,128)(2,1)} %param.11) | copy-start | bytes 6291460
  967.0 6.2 copy-start.18
  973.2 56.9 %copy-start.4 = (bf16[256,4096]{1,0:T(8,128)(2,1)}, bf16[256,4096]{1,0:T(8,128)(2,1)S(1)}, u32[]{:S(2)}) copy-start(bf16[256,4096]{1,0:T(8,128)(2,1)S(1)} %get-tuple-element.10) | copy-start | bytes 6291460
  998.2 60.7 %collective-permute-start.1 = (f32[127,4096]{1,0:T(8,128)}, f32[127,4096]{1,0:T(8,128)}, u32[]{:S(2)}, u32[]{:S(2)}) collective-permute-start(f32[127,4096]{1,0:T(8,128)} %copy.123), channel_id=1, source_target_pairs={{1,0},{2,1},{3,2},{4,3},{5,4},{6,5},{7,6},{8,7},{9,8},{10,9},{11,1... | collective-permute-start | bytes 6242312 | tf_op jit(solution)/shard_map/ppermute | solution.py:32
  1054.5 4.4 copy-start.6
  1054.5 4.4 copy-start.7
  1059.0 124.3 %copy-start.1 = (bf16[1,256,4096]{2,1,0:T(8,128)(2,1)S(1)}, bf16[1,256,4096]{2,1,0:T(8,128)(2,1)}, u32[]{:S(2)}) copy-start(bf16[1,256,4096]{2,1,0:T(8,128)(2,1)} %param.14) | copy-start | bytes 6291460
  (3 other events, 9.1 us)
Sparse Core Ops, SparseCore 0:
  19.7 28.5 all-gather.2
  193.5 33.8 reduce-scatter.4
  229.0 720.7 all-gather.4
  1002.9 142.2 reduce-scatter.2
